TPU v7x, 32 devices: a whole 2x2x4 slice. The times are simulated.
32 devices in a mesh: work: 8 (over z, y), firm: 4 (over x, core).
Axes of the slice: x: 2, y: 2, z: 4, core: 2. Of those that a mesh axis runs over, the one named last changes fastest.
Arguments:
- worker_feat: bfloat16 [64, 16384], P('firm', 'work'), may hold values from -4 to 4
- firm_feat: bfloat16 [64, 16384], P('work', 'firm'), may hold values from -1.75 to 1.75
- worker_pot: float32 [16384], P('work'), may hold values from -1 to 1
- firm_pot: float32 [16384], P('firm'), may hold values from -1 to 1
- worker_caps: int32 [16384], P('work'), may hold values from 1 to 5
- firm_caps: int32 [16384], P('firm'), may hold values from 1 to 5
Outputs:
- step_workers: float32 [16384], P('work')
- step_firms: float32 [16384], P('firm')
All inputs are finite; a program needn't handle non-finite values.
Results may differ from a plain program's by a relative error of at most 0.0003.
Values may be sent and summed in bfloat16 or wider, within the bound.
A program may use at most 64 MiB of HBM per device.

v0:
```python
import math
import jax
import jax.numpy as jnp
from jax import lax
from jax.sharding import PartitionSpec as P

ITERS = 4


def body(worker_feat, firm_feat, worker_pot, firm_pot, worker_caps, firm_caps):
    wfeat = lax.all_gather(worker_feat, "firm", axis=0, tiled=True)
    ffeat = lax.all_gather(firm_feat, "work", axis=0, tiled=True)
    rows_here = wfeat.shape[1]
    cols_here = ffeat.shape[1]
    inverse = 1.0 / (cols_here * lax.axis_size("firm"))
    scale = 1.0 / math.sqrt(wfeat.shape[0])
    width = 256
    blocks = cols_here // width
    first_firm = lax.axis_index("firm") == 0
    first_work = lax.axis_index("work") == 0

    def kernel_pass(vec_u, vec_v):

        def step(rows_acc, index):
            start = index * width
            feat_blk = lax.dynamic_slice_in_dim(ffeat, start, width, 1)
            pot_blk = lax.dynamic_slice_in_dim(firm_pot, start, width, 0)
            vec_blk = lax.dynamic_slice_in_dim(vec_v, start, width, 0)
            surplus = lax.dot_general(
                wfeat, feat_blk, (((0,), (0,)), ((), ())), preferred_element_type=jnp.float32
            )
            kernel = jnp.exp(surplus * scale - worker_pot[:, None] - pot_blk[None, :]) * inverse
            rows_acc = rows_acc + jnp.dot(kernel, vec_blk, precision=lax.Precision.HIGHEST)
            col_blk = jnp.dot(vec_u, kernel, precision=lax.Precision.HIGHEST)
            return (rows_acc, col_blk)

        rows_part, col_blocks = lax.scan(
            step, jnp.zeros((rows_here,), jnp.float32), jnp.arange(blocks, dtype=jnp.int32)
        )
        rows_full = lax.psum(rows_part, "firm")
        cols_part = col_blocks.reshape(cols_here)
        cols = lax.psum(cols_part, "work")
        return (rows_full, cols)

    row_total, col_total = kernel_pass(
        jnp.ones((rows_here,), jnp.float32), jnp.ones((cols_here,), jnp.float32)
    )
    diag_u = row_total + jnp.exp(-worker_pot)
    diag_v = col_total + jnp.exp(-firm_pot)
    rhs_u = diag_u - worker_caps.astype(jnp.float32)
    rhs_v = diag_v - firm_caps.astype(jnp.float32)

    def hessian(dir_u, dir_v):
        prod_u, prod_v = kernel_pass(dir_u, dir_v)
        return (diag_u * dir_u + prod_u, diag_v * dir_v + prod_v)

    def local_dot(left_u, left_v, right_u, right_v):
        part_u = jnp.where(first_firm, jnp.sum(left_u * right_u), 0.0)
        part_v = jnp.where(first_work, jnp.sum(left_v * right_v), 0.0)
        return part_u + part_v

    step_u = jnp.zeros_like(rhs_u)
    step_v = jnp.zeros_like(rhs_v)
    res_u, res_v = (rhs_u, rhs_v)

    def two_products(left_u, left_v, image_u, image_v):
        return lax.psum(
            (
                local_dot(left_u, left_v, left_u, left_v),
                local_dot(left_u, left_v, image_u, image_v),
            ),
            ("work", "firm"),
        )

    image_u, image_v = hessian(res_u, res_v)
    norm_now, product = two_products(res_u, res_v, image_u, image_v)
    alpha = norm_now / product
    dir_u, dir_v = (res_u, res_v)
    along_u, along_v = (image_u, image_v)
    for index in range(ITERS):
        step_u = step_u + alpha * dir_u
        step_v = step_v + alpha * dir_v
        if index + 1 < ITERS:
            res_u = res_u - alpha * along_u
            res_v = res_v - alpha * along_v
            image_u, image_v = hessian(res_u, res_v)
            norm_next, product = two_products(res_u, res_v, image_u, image_v)
            ratio = norm_next / norm_now
            alpha = norm_next / (product - ratio * norm_next / alpha)
            dir_u = res_u + ratio * dir_u
            dir_v = res_v + ratio * dir_v
            along_u = image_u + ratio * along_u
            along_v = image_v + ratio * along_v
            norm_now = norm_next
    return (step_u, step_v)


def solution(mesh):
    placed = (P("firm", "work"), P("work", "firm"), P("work"), P("firm"), P("work"), P("firm"))
    return jax.shard_map(
        body, mesh=mesh, in_specs=placed, out_specs=(P("work"), P("firm")), check_vma=False
    )
```

profile of v0, /device:TPU:12, one launch (start us, length us, event | category | flops | bytes accessed | tf_op | source)
XLA Modules:
  0.0 947.6 jit_solution(16463058012622074813)
XLA Ops:
  0.7 29.7 %all_gather.6 = bf16[64,4096]{1,0:T(8,128)(2,1)S(1)} all-gather(bf16[8,4096]{1,0:T(8,128)(2,1)} %param.17), channel_id=1, replica_groups=mesh['work'=8,'firm'=4] {'work'}, dimensions={0}, use_global_device_ids=true | all-gather | bytes 589824 | tf_op jit(solution)/shard_map/all_gather | solution.py:12
  30.3 6.0 all_gather.7
  36.3 103.3 %while.65 = (s32[]{:T(128)}, f32[2048]{0:T(1024)S(1)}, f32[16,256]{1,0:T(8,128)S(1)}, s32[16]{0:T(128)S(1)}, bf16[64,4096]{1,0:T(8,128)(2,1)S(1)}, /*index=5*/bf...) while((s32[]{:T(128)}, f32[2048]{0:T(1024)S(1)}, ...), condition=%wide.region_1.2_spmd.clone, body=%wide.region_0.1_spmd.clone.sunk | while | flops 81793032 | bytes 6633677 | solution.py:37
  139.6 32.1 %psum.127 = f32[4096]{0:T(1024)S(1)} all-reduce(f32[4096]{0:T(1024)S(1)} %bitcast.176), channel_id=1, replica_groups=mesh['work'=8,'firm'=4] {'work'}, use_global_device_ids=true, to_apply=%region_4.5 | all-reduce | flops 4096 | bytes 32768 | tf_op jit(solution)/shard_map/psum | solution.py:42
  172.5 5.8 psum.126
  179.0 104.5 %while.66 = (s32[]{:T(128)}, f32[2048]{0:T(1024)S(1)}, f32[16,256]{1,0:T(8,128)S(1)}, s32[16]{0:T(128)S(1)}, bf16[64,4096]{1,0:T(8,128)(2,1)S(1)}, /*index=5*/bf...) while((s32[]{:T(128)}, f32[2048]{0:T(1024)S(1)}, ...), condition=%wide.region_8.9_spmd.clone, body=%wide.region_7.8_spmd.clone.sunk | while | flops 81793032 | bytes 6644961 | solution.py:37
  183.7 1.7 fusion.134
  190.3 1.7 fusion.134
  196.8 1.7 fusion.134
  203.3 1.7 fusion.134
  209.8 1.7 fusion.134
  216.4 1.7 fusion.134
  222.9 1.7 fusion.134
  229.4 1.7 fusion.134
  283.4 6.7 psum.129
  291.5 36.0 %psum.130 = f32[4096]{0:T(1024)S(1)} all-reduce(f32[4096]{0:T(1024)S(1)} %bitcast.177), channel_id=1, replica_groups=mesh['work'=8,'firm'=4] {'work'}, use_global_device_ids=true, to_apply=%region_11.12 | all-reduce | flops 4096 | bytes 32768 | tf_op jit(solution)/shard_map/psum | solution.py:42
  330.2 43.5 %all-reduce.3 = (f32[]{:T(128)}, f32[]{:T(128)}) all-reduce(f32[]{:T(128)S(6)} %add.194, f32[]{:T(128)S(6)} %add.197), channel_id=1, replica_groups=mesh['work'=8,'firm'=4] {'work','firm'}, use_global_device_ids=true, to_apply=%region_6.7 | all-reduce | flops 2 | bytes 16 | tf_op jit(solution)/shard_map/psum | solution.py:67
  375.1 101.1 %while.67 = (s32[]{:T(128)}, f32[2048]{0:T(1024)S(1)}, f32[16,256]{1,0:T(8,128)S(1)}, s32[16]{0:T(128)S(1)}, bf16[64,4096]{1,0:T(8,128)(2,1)S(1)}, /*index=5*/bf...) while((s32[]{:T(128)}, f32[2048]{0:T(1024)S(1)}, ...), condition=%wide.region_18.19_spmd.clone, body=%wide.region_17.18_spmd.clone.sunk | while | flops 81793032 | bytes 6644961 | solution.py:37
  385.9 1.7 fusion.143
  417.5 1.7 fusion.143
  476.1 5.8 psum.133
  483.1 27.5 %psum.134 = f32[4096]{0:T(1024)S(1)} all-reduce(f32[4096]{0:T(1024)S(1)} %bitcast.178), channel_id=1, replica_groups=mesh['work'=8,'firm'=4] {'work'}, use_global_device_ids=true, to_apply=%region_21.22 | all-reduce | flops 4096 | bytes 32768 | tf_op jit(solution)/shard_map/psum | solution.py:42
  513.1 46.4 %all-reduce.2 = (f32[]{:T(128)}, f32[]{:T(128)}) all-reduce(f32[]{:T(128)S(6)} %add.198, f32[]{:T(128)S(6)} %add.201), channel_id=1, replica_groups=mesh['work'=8,'firm'=4] {'work','firm'}, use_global_device_ids=true, to_apply=%region_16.17 | all-reduce | flops 2 | bytes 16 | tf_op jit(solution)/shard_map/psum | solution.py:67
  564.0 102.5 %while.68 = (s32[]{:T(128)}, f32[2048]{0:T(1024)S(1)}, f32[16,256]{1,0:T(8,128)S(1)}, s32[16]{0:T(128)S(1)}, bf16[64,4096]{1,0:T(8,128)(2,1)S(1)}, /*index=5*/bf...) while((s32[]{:T(128)}, f32[2048]{0:T(1024)S(1)}, ...), condition=%wide.region_28.29_spmd.clone, body=%wide.region_27.28_spmd.clone.sunk | while | flops 81793032 | bytes 6644961 | solution.py:37
  619.9 1.7 fusion.152
  666.5 5.8 psum.137
  673.6 27.5 %psum.138 = f32[4096]{0:T(1024)S(1)} all-reduce(f32[4096]{0:T(1024)S(1)} %bitcast.179), channel_id=1, replica_groups=mesh['work'=8,'firm'=4] {'work'}, use_global_device_ids=true, to_apply=%region_31.32 | all-reduce | flops 4096 | bytes 32768 | tf_op jit(solution)/shard_map/psum | solution.py:42
  703.8 46.4 %all-reduce.1 = (f32[]{:T(128)}, f32[]{:T(128)}) all-reduce(f32[]{:T(128)S(6)} %add.206, f32[]{:T(128)S(6)} %add.209), channel_id=1, replica_groups=mesh['work'=8,'firm'=4] {'work','firm'}, use_global_device_ids=true, to_apply=%region_26.27 | all-reduce | flops 2 | bytes 16 | tf_op jit(solution)/shard_map/psum | solution.py:67
  754.1 104.5 %while.69 = (s32[]{:T(128)}, f32[2048]{0:T(1024)S(1)}, f32[16,256]{1,0:T(8,128)S(1)}, s32[16]{0:T(128)S(1)}, bf16[64,4096]{1,0:T(8,128)(2,1)S(1)}, /*index=5*/bf...) while((s32[]{:T(128)}, f32[2048]{0:T(1024)S(1)}, ...), condition=%wide.region_38.39_spmd.clone, body=%wide.region_37.38_spmd.clone.sunk | while | flops 81793032 | bytes 6644961 | solution.py:37
  858.5 5.8 psum.141
  865.7 27.5 %psum.142 = f32[4096]{0:T(1024)S(1)} all-reduce(f32[4096]{0:T(1024)S(1)} %bitcast.180), channel_id=1, replica_groups=mesh['work'=8,'firm'=4] {'work'}, use_global_device_ids=true, to_apply=%region_41.42 | all-reduce | flops 4096 | bytes 32768 | tf_op jit(solution)/shard_map/psum | solution.py:42
  895.8 46.5 %all-reduce = (f32[]{:T(128)}, f32[]{:T(128)}) all-reduce(f32[]{:T(128)S(6)} %add.214, f32[]{:T(128)S(6)} %add.217), channel_id=1, replica_groups=mesh['work'=8,'firm'=4] {'work','firm'}, use_global_device_ids=true, to_apply=%region_36.37 | all-reduce | flops 2 | bytes 16 | tf_op jit(solution)/shard_map/psum | solution.py:67
  (655 shorter events, 449.0 us)
Async XLA Ops:
  36.3 135.4 %copy-start = (s32[4096]{0:T(1024)S(1)}, s32[4096]{0:T(1024)}, u32[]{:S(2)}) copy-start(s32[4096]{0:T(1024)} %param.21) | copy-start | bytes 49156
  36.3 141.9 %copy-start.1 = (s32[2048]{0:T(1024)S(1)}, s32[2048]{0:T(1024)}, u32[]{:S(2)}) copy-start(s32[2048]{0:T(1024)} %param.20) | copy-start | bytes 24580
where the time goes:
time: 957 us; the launch traced here: 948 us
  blocking collectives  399 us (42%)
  matrix products  340 us (36%)
  local copies, waits for them, and re-layouts  120 us (13%)
  loops' own time  55.9 us (6%)
  between operations  24.8 us (3%)
    psum x4, blocking collectives, two_products(): lax.psum((local_dot(left_u, left_v, left_u, left_v), local_dot(left_u, le...  183 us
    psum x5, blocking collectives, kernel_pass(): cols = lax.psum(cols_part, 'work')  151 us
    dot_general x80, matrix products, step(): col_blk = jnp.dot(vec_u, kernel, precision=lax.Precision.HIGHEST)  138 us
    dot_general x80, matrix products, step(): lax.dot_general(wfeat, feat_blk, (((0,), (0,)), ((), ())), preferred_elem...  106 us
    dot_general x80, matrix products, step(): jnp.dot(kernel, vec_blk, precision=lax.Precision.HIGHEST)  94.9 us
    dynamic_slice x80, local copies, waits for them, and re-layouts, step(): pot_blk = lax.dynamic_slice_in_dim(firm_pot, start, width, 0)  61.2 us
    another operation x5, loops' own time, kernel_pass(): lax.scan(step, jnp.zeros((rows_here,), jnp.float32), jnp.arange(blocks, d...  55.9 us
    dynamic_slice x80, local copies, waits for them, and re-layouts, kernel_pass(): lax.scan(step, jnp.zeros((rows_here,), jnp.float32), jnp.arange(blocks, d...  50.6 us

commit v1 on v0

--- a/solution.py
+++ b/solution.py
@@ -1,3 +1,4 @@
+import functools
 import math
 import jax
 import jax.numpy as jnp
@@ -7,9 +8,37 @@
 ITERS = 4
 
 
+def wall_produce(values, named_axis):
+    small, heard, work_now = (
+        lax.axis_size(named_axis),
+        lax.axis_index(named_axis),
+        values.shape[0],
+    )
+    fields = list(map(lambda h: (h, (h + 1) % small), range(small)))
+    tray = list(map(lambda h: (h, (h - 1) % small), range(small)))
+    seen_now = jnp.zeros((*values.shape[:0], small * work_now, *values.shape[1:]), values.dtype)
+    seen_now = lax.dynamic_update_slice_in_dim(seen_now, values, heard * work_now, axis=0)
+    res = small // 2
+    d_next = ready = values
+    for ii in range(1, res + 1):
+        d_next = lax.ppermute(d_next, axis_name=named_axis, perm=fields)
+        seen_now = lax.dynamic_update_slice_in_dim(
+            seen_now, d_next, (heard - ii) % small * work_now, axis=0
+        )
+        if ii < small - res:
+            ready = lax.ppermute(ready, axis_name=named_axis, perm=tray)
+            seen_now = lax.dynamic_update_slice_in_dim(
+                seen_now, ready, (heard + ii) % small * work_now, axis=0
+            )
+    return seen_now
+
+
+measure_knots_in = functools.partial(wall_produce, named_axis="work")
+
+
 def body(worker_feat, firm_feat, worker_pot, firm_pot, worker_caps, firm_caps):
     wfeat = lax.all_gather(worker_feat, "firm", axis=0, tiled=True)
-    ffeat = lax.all_gather(firm_feat, "work", axis=0, tiled=True)
+    ffeat = measure_knots_in(firm_feat)
     rows_here = wfeat.shape[1]
     cols_here = ffeat.shape[1]
     inverse = 1.0 / (cols_here * lax.axis_size("firm"))

time: 957 us -> 827 us (0.86)
  matrix products: 340 us -> 284 us
  local copies, waits for them, and re-layouts: 120 us -> 65.3 us
  blocking collectives: 399 us -> 372 us
  starting transfers between devices: 0 us -> 11.6 us
    dot_general x80, matrix products: 106 us -> 51.3 us  [step(): lax.dot_general(wfeat, feat_blk, (((0,), (0,)), ((), ())), preferred_elem...]
    dynamic_slice x80, local copies, waits for them, and re-layouts: 61.2 us -> 6.3 us  [step(): pot_blk = lax.dynamic_slice_in_dim(firm_pot, start, width, 0)]
    all_gather x1 -> x0, blocking collectives: 29.7 us -> none  [body(): ffeat = lax.all_gather(firm_feat, 'work', axis=0, tiled=True)]
    ppermute x0 -> x7, starting transfers between devices: none -> 11.6 us  [the longest x4 10.8 us: wall_produce(): d_next = lax.ppermute(d_next, axis_name=named_axis, perm=fields)]
  transfers between devices with their start and end apart: 0 -> 7, of which waited for: 0 -> 3; matrix products, arithmetic and copies ran while one was open for 0% -> 0% of each run, Pallas kernels for 0% -> 0%
where the time goes in v1:
time: 827 us; the launch traced here: 824 us
  blocking collectives  372 us (45%)
  matrix products  284 us (34%)
  local copies, waits for them, and re-layouts  65.3 us (8%)
  loops' own time  53.9 us (7%)
  between operations  24.8 us (3%)
  starting transfers between devices  11.6 us (1%)
    psum x4, blocking collectives, two_products(): lax.psum((local_dot(left_u, left_v, left_u, left_v), local_dot(left_u, le...  183 us
    psum x5, blocking collectives, kernel_pass(): cols = lax.psum(cols_part, 'work')  153 us
    dot_general x80, matrix products, step(): col_blk = jnp.dot(vec_u, kernel, precision=lax.Precision.HIGHEST)  138 us
    dot_general x80, matrix products, step(): jnp.dot(kernel, vec_blk, precision=lax.Precision.HIGHEST)  94.9 us
    another operation x5, loops' own time, kernel_pass(): lax.scan(step, jnp.zeros((rows_here,), jnp.float32), jnp.arange(blocks, d...  53.9 us
    dot_general x80, matrix products, step(): lax.dot_general(wfeat, feat_blk, (((0,), (0,)), ((), ())), preferred_elem...  51.3 us
    dynamic_slice x80, local copies, waits for them, and re-layouts, kernel_pass(): lax.scan(step, jnp.zeros((rows_here,), jnp.float32), jnp.arange(blocks, d...  49.9 us
    psum x5, blocking collectives, kernel_pass(): rows_full = lax.psum(rows_part, 'firm')  29.8 us
  transfers between devices with their start and end apart: 7, of which 3 were waited for; matrix products, arithmetic and copies ran while one was open for 0% of the time, Pallas kernels for 0%

profile of v1, /device:TPU:12, one launch (start us, length us, event | category | flops | bytes accessed | tf_op | source)
XLA Modules:
  0.0 824.3 jit_solution(3296113879459534357)
XLA Ops:
  3.6 6.0 all_gather.3
  9.6 2.4 collective-permute-start.2
  12.1 1.9 collective-permute-done.2
  14.0 3.4 collective-permute-start.4
  19.3 3.4 collective-permute-start.6
  22.7 1.9 collective-permute-done.6
  24.6 79.5 %while.65 = (s32[]{:T(128)}, f32[2048]{0:T(1024)S(1)}, f32[16,256]{1,0:T(8,128)S(1)}, s32[16]{0:T(128)S(1)}, bf16[64,4096]{1,0:T(8,128)(2,1)S(1)}, /*index=5*/bf...) while((s32[]{:T(128)}, f32[2048]{0:T(1024)S(1)}, ...), condition=%wide.region_1.2_spmd.clone, body=%wide.region_0.1_spmd.clone.sunk | while | flops 81793032 | bytes 6633677 | solution.py:66
  104.2 37.4 %psum.127 = f32[4096]{0:T(1024)S(1)} all-reduce(f32[4096]{0:T(1024)S(1)} %bitcast.176), channel_id=1, replica_groups=mesh['work'=8,'firm'=4] {'work'}, use_global_device_ids=true, to_apply=%region_4.5 | all-reduce | flops 4096 | bytes 32768 | tf_op jit(solution)/shard_map/psum | solution.py:71
  141.6 5.7 psum.126
  147.4 80.8 %while.66 = (s32[]{:T(128)}, f32[2048]{0:T(1024)S(1)}, f32[16,256]{1,0:T(8,128)S(1)}, s32[16]{0:T(128)S(1)}, bf16[64,4096]{1,0:T(8,128)(2,1)S(1)}, /*index=5*/bf...) while((s32[]{:T(128)}, f32[2048]{0:T(1024)S(1)}, ...), condition=%wide.region_8.9_spmd.clone, body=%wide.region_7.8_spmd.clone.sunk | while | flops 81793032 | bytes 6644961 | solution.py:66
  150.7 1.7 fusion.134
  155.7 1.7 fusion.134
  160.8 1.7 fusion.134
  165.8 1.7 fusion.134
  170.9 1.7 fusion.134
  228.2 6.7 psum.129
  234.9 33.0 %psum.130 = f32[4096]{0:T(1024)S(1)} all-reduce(f32[4096]{0:T(1024)S(1)} %bitcast.177), channel_id=1, replica_groups=mesh['work'=8,'firm'=4] {'work'}, use_global_device_ids=true, to_apply=%region_11.12 | all-reduce | flops 4096 | bytes 32768 | tf_op jit(solution)/shard_map/psum | solution.py:71
  271.7 43.5 %all-reduce.3 = (f32[]{:T(128)}, f32[]{:T(128)}) all-reduce(f32[]{:T(128)S(6)} %add.271, f32[]{:T(128)S(6)} %add.274), channel_id=1, replica_groups=mesh['work'=8,'firm'=4] {'work','firm'}, use_global_device_ids=true, to_apply=%region_6.7 | all-reduce | flops 2 | bytes 16 | tf_op jit(solution)/shard_map/psum | solution.py:96
  316.5 81.3 %while.67 = (s32[]{:T(128)}, f32[2048]{0:T(1024)S(1)}, f32[16,256]{1,0:T(8,128)S(1)}, s32[16]{0:T(128)S(1)}, bf16[64,4096]{1,0:T(8,128)(2,1)S(1)}, /*index=5*/bf...) while((s32[]{:T(128)}, f32[2048]{0:T(1024)S(1)}, ...), condition=%wide.region_18.19_spmd.clone, body=%wide.region_17.18_spmd.clone.sunk | while | flops 81793032 | bytes 6644961 | solution.py:66
  319.8 1.7 fusion.143
  397.9 5.8 psum.133
  404.4 27.5 %psum.134 = f32[4096]{0:T(1024)S(1)} all-reduce(f32[4096]{0:T(1024)S(1)} %bitcast.178), channel_id=1, replica_groups=mesh['work'=8,'firm'=4] {'work'}, use_global_device_ids=true, to_apply=%region_21.22 | all-reduce | flops 4096 | bytes 32768 | tf_op jit(solution)/shard_map/psum | solution.py:71
  435.1 46.5 %all-reduce.2 = (f32[]{:T(128)}, f32[]{:T(128)}) all-reduce(f32[]{:T(128)S(6)} %add.275, f32[]{:T(128)S(6)} %add.278), channel_id=1, replica_groups=mesh['work'=8,'firm'=4] {'work','firm'}, use_global_device_ids=true, to_apply=%region_16.17 | all-reduce | flops 2 | bytes 16 | tf_op jit(solution)/shard_map/psum | solution.py:96
  486.1 79.0 %while.68 = (s32[]{:T(128)}, f32[2048]{0:T(1024)S(1)}, f32[16,256]{1,0:T(8,128)S(1)}, s32[16]{0:T(128)S(1)}, bf16[64,4096]{1,0:T(8,128)(2,1)S(1)}, /*index=5*/bf...) while((s32[]{:T(128)}, f32[2048]{0:T(1024)S(1)}, ...), condition=%wide.region_28.29_spmd.clone, body=%wide.region_27.28_spmd.clone.sunk | while | flops 81793032 | bytes 6644961 | solution.py:66
  514.0 1.7 fusion.152
  565.2 5.8 psum.137
  571.6 27.5 %psum.138 = f32[4096]{0:T(1024)S(1)} all-reduce(f32[4096]{0:T(1024)S(1)} %bitcast.179), channel_id=1, replica_groups=mesh['work'=8,'firm'=4] {'work'}, use_global_device_ids=true, to_apply=%region_31.32 | all-reduce | flops 4096 | bytes 32768 | tf_op jit(solution)/shard_map/psum | solution.py:71
  602.3 46.6 %all-reduce.1 = (f32[]{:T(128)}, f32[]{:T(128)}) all-reduce(f32[]{:T(128)S(6)} %add.283, f32[]{:T(128)S(6)} %add.286), channel_id=1, replica_groups=mesh['work'=8,'firm'=4] {'work','firm'}, use_global_device_ids=true, to_apply=%region_26.27 | all-reduce | flops 2 | bytes 16 | tf_op jit(solution)/shard_map/psum | solution.py:96
  652.9 82.5 %while.69 = (s32[]{:T(128)}, f32[2048]{0:T(1024)S(1)}, f32[16,256]{1,0:T(8,128)S(1)}, s32[16]{0:T(128)S(1)}, bf16[64,4096]{1,0:T(8,128)(2,1)S(1)}, /*index=5*/bf...) while((s32[]{:T(128)}, f32[2048]{0:T(1024)S(1)}, ...), condition=%wide.region_38.39_spmd.clone, body=%wide.region_37.38_spmd.clone.sunk | while | flops 81793032 | bytes 6644961 | solution.py:66
  735.4 5.8 psum.141
  741.9 27.5 %psum.142 = f32[4096]{0:T(1024)S(1)} all-reduce(f32[4096]{0:T(1024)S(1)} %bitcast.180), channel_id=1, replica_groups=mesh['work'=8,'firm'=4] {'work'}, use_global_device_ids=true, to_apply=%region_41.42 | all-reduce | flops 4096 | bytes 32768 | tf_op jit(solution)/shard_map/psum | solution.py:71
  772.6 46.5 %all-reduce = (f32[]{:T(128)}, f32[]{:T(128)}) all-reduce(f32[]{:T(128)S(6)} %add.291, f32[]{:T(128)S(6)} %add.294), channel_id=1, replica_groups=mesh['work'=8,'firm'=4] {'work','firm'}, use_global_device_ids=true, to_apply=%region_36.37 | all-reduce | flops 2 | bytes 16 | tf_op jit(solution)/shard_map/psum | solution.py:96
  (681 shorter events, 348.7 us)
Async XLA Ops:
  0.6 24.0 %copy-start.3 = (f32[2048]{0:T(1024)S(1)}, f32[2048]{0:T(1024)}, u32[]{:S(2)}) copy-start(f32[2048]{0:T(1024)} %param.18) | copy-start | bytes 24580
  0.6 24.0 %copy-start = (f32[4096]{0:T(1024)S(1)}, f32[4096]{0:T(1024)}, u32[]{:S(2)}) copy-start(f32[4096]{0:T(1024)} %param.19) | copy-start | bytes 49156
  0.6 9.0 %collective-permute-start = (bf16[8,4096]{1,0:T(8,128)(2,1)}, bf16[8,4096]{1,0:T(8,128)(2,1)S(1)}, u32[]{:S(2)}, u32[]{:S(2)}) collective-permute-start(bf16[8,4096]{1,0:T(8,128)(2,1)} %param.17), channel_id=1, source_target_pairs={{0,4},{4,8},{8,12},{12,16},{16,20},{20,24},{24,28},{28,0},{1,5},{5... | collective-permute-start | bytes 196616 | tf_op jit(solution)/shard_map/ppermute | solution.py:24
  2.2 9.8 %collective-permute-start.1 = (bf16[8,4096]{1,0:T(8,128)(2,1)}, bf16[8,4096]{1,0:T(8,128)(2,1)S(1)}, u32[]{:S(2)}, u32[]{:S(2)}) collective-permute-start(bf16[8,4096]{1,0:T(8,128)(2,1)} %param.17), channel_id=1, source_target_pairs={{0,28},{4,0},{8,4},{12,8},{16,12},{20,16},{24,20},{28,24},{1,29},{... | collective-permute-start | bytes 196616 | tf_op jit(solution)/shard_map/ppermute | solution.py:29
  9.6 4.3 collective-permute-start.2
  12.1 5.3 collective-permute-start.3
  14.0 5.3 collective-permute-start.4
  17.4 5.3 collective-permute-start.5
  19.3 5.3 collective-permute-start.6
  24.6 122.7 %copy-start.1 = (s32[4096]{0:T(1024)S(1)}, s32[4096]{0:T(1024)}, u32[]{:S(2)}) copy-start(s32[4096]{0:T(1024)} %param.21) | copy-start | bytes 49156
  24.6 122.7 %copy-start.2 = (s32[2048]{0:T(1024)S(1)}, s32[2048]{0:T(1024)}, u32[]{:S(2)}) copy-start(s32[2048]{0:T(1024)} %param.20) | copy-start | bytes 24580
